TPU v7x, 512 devices: a whole 4x8x8 slice. The times are simulated.
512 devices in a mesh: seq: 64 (over y, x, core), tensor: 8 (over z).
Axes of the slice: x: 4, y: 8, z: 8, core: 2. Of those that a mesh axis runs over, the one named last changes fastest.
Arguments:
- query_rows: bfloat16 [8192, 4096], P('seq', 'tensor'), may hold values from -6 to 6
- key_rows: bfloat16 [8192, 4096], P('seq', 'tensor'), may hold values from -6 to 6
- value_rows: bfloat16 [8192, 4096], P('seq', 'tensor'), may hold values from -18 to 18
- cluster_id: int32 [32, 8192], P('tensor', 'seq'), may hold values from 0 to 511, as said below
- slot_index: int32 [32, 8192], P('tensor', 'seq'), may hold values from 0 to 31, as said below
- out_weight: bfloat16 [4096, 2048], P('tensor', 'seq'), may hold values from -0.09375 to 0.09375
- grad_out: bfloat16 [8192, 2048], P(('seq', 'tensor')), may hold values from -6 to 6
Outputs:
- mixed: bfloat16 [8192, 2048], P(('seq', 'tensor'))
- grad_query: bfloat16 [8192, 4096], P('seq', 'tensor')
- grad_key: bfloat16 [8192, 4096], P('seq', 'tensor')
- grad_value: bfloat16 [8192, 4096], P('seq', 'tensor')
Inputs may be any that keep to these rules, and one draw needn't show every extreme that they name: `cluster_id`: cluster c of a head belongs to the index c // 8 of seq. Each cluster of a head holds at most 32 tokens and in every head some cluster holds exactly 32. The tokens of one index of seq go, for one head, to at most 4 slots among the clusters of one owner, and every index of seq reaches 4 for some owner in every head. `slot_index`: within one head and cluster the slots of its tokens are distinct.
All inputs are finite; a program needn't handle non-finite values.
Results may differ from a plain program's by a relative error of at most 0.025.
Values may be sent and summed in bfloat16 or wider, within the bound.
A program may use at most 64 MiB of HBM per device.

v0:
```python
import math

import jax
import jax.numpy as jnp
from jax import lax
from jax.sharding import PartitionSpec as P

CLU_DEV = 8
CAP = 32


def shards(query_rows, key_rows, value_rows, cluster_id, slot_index, out_weight, grad_out):
    rows_dev = query_rows.shape[0]
    heads_dev = cluster_id.shape[0]
    head_size = query_rows.shape[1] // heads_dev
    owners = lax.axis_size("seq")
    send_most = 2 * rows_dev // owners
    buffer_rows = owners * send_most
    room = CLU_DEV * CAP
    score_scale = 1.0 / math.sqrt(head_size)
    masked_score = -1e30
    owner = cluster_id // CLU_DEV
    owner_onehot = (owner[:, :, None] == jnp.arange(owners, dtype=jnp.int32)[None, None, :]).astype(
        jnp.bfloat16
    )
    row_ids = jnp.arange(rows_dev, dtype=jnp.int32)
    lower = (row_ids[:, None] > row_ids[None, :]).astype(jnp.bfloat16)
    earlier = jnp.einsum("ij,hjo->hio", lower, owner_onehot, preferred_element_type=jnp.float32)
    rank = jnp.sum(earlier * owner_onehot.astype(jnp.float32), axis=2).astype(jnp.int32)
    place = owner * send_most + rank
    target = cluster_id % CLU_DEV * CAP + slot_index
    buffer_ids = jnp.arange(buffer_rows, dtype=jnp.int32)
    send_table = (place[:, None, :] == buffer_ids[None, :, None]).astype(jnp.bfloat16)

    def to_buffer(rows):
        split = rows.reshape(rows_dev, heads_dev, head_size)
        filled = jnp.einsum(
            "hbi,ihd->bhd", send_table, split, preferred_element_type=jnp.float32
        ).astype(rows.dtype)
        return filled.reshape(buffer_rows, heads_dev * head_size)

    def from_buffer(buffer):
        split = buffer.reshape(buffer_rows, heads_dev, head_size)
        picked = jnp.einsum(
            "hbi,bhd->ihd", send_table, split, preferred_element_type=jnp.float32
        ).astype(buffer.dtype)
        return picked.reshape(rows_dev, heads_dev * head_size)

    target_rows = (
        jnp.einsum(
            "hbi,hi->bh", send_table.astype(jnp.float32), (target - room).astype(jnp.float32)
        ).astype(jnp.int32)
        + room
    )
    arrived = lax.all_to_all(target_rows, "seq", split_axis=0, concat_axis=0, tiled=True)
    routed_query, routed_key, routed_value = (
        lax.all_to_all(to_buffer(query_rows), "seq", split_axis=0, concat_axis=0, tiled=True),
        lax.all_to_all(to_buffer(key_rows), "seq", split_axis=0, concat_axis=0, tiled=True),
        lax.all_to_all(to_buffer(value_rows), "seq", split_axis=0, concat_axis=0, tiled=True),
    )
    room_ids = jnp.arange(room, dtype=jnp.int32)
    cell_table = (arrived.T[:, None, :] == room_ids[None, :, None]).astype(jnp.bfloat16)

    def to_cells(buffer):
        split = buffer.reshape(buffer_rows, heads_dev, head_size)
        cells = jnp.einsum(
            "hrb,bhd->hrd", cell_table, split, preferred_element_type=jnp.float32
        ).astype(buffer.dtype)
        return cells.reshape(heads_dev, CLU_DEV, CAP, head_size)

    def to_returns(cells):
        flat = cells.reshape(heads_dev, room, head_size)
        picked = jnp.einsum(
            "hrb,hrd->bhd", cell_table, flat, preferred_element_type=jnp.float32
        ).astype(cells.dtype)
        return picked.reshape(buffer_rows, heads_dev * head_size)

    live = jnp.sum(cell_table.astype(jnp.float32), axis=2).reshape(heads_dev, CLU_DEV, CAP)
    query_cells = to_cells(routed_query)
    key_cells = to_cells(routed_key)
    value_cells = to_cells(routed_value)
    scores = (
        jnp.einsum("hcqd,hckd->hcqk", query_cells, key_cells, preferred_element_type=jnp.float32)
        * score_scale
    )
    scores = jnp.where(live[:, :, None, :] > 0.5, scores, masked_score)
    top = jnp.max(scores, axis=-1, keepdims=True)
    weights = jnp.exp(scores - top)
    probs = weights / jnp.sum(weights, axis=-1, keepdims=True)
    probs_low = probs.astype(jnp.bfloat16)
    attended_cells = jnp.einsum(
        "hcqk,hckd->hcqd", probs_low, value_cells, preferred_element_type=jnp.float32
    ).astype(jnp.bfloat16)
    returned = lax.all_to_all(
        to_returns(attended_cells), "seq", split_axis=0, concat_axis=0, tiled=True
    )
    attended = from_buffer(returned)
    full_weight = lax.all_gather(out_weight, "seq", axis=1, tiled=True)
    rows = attended
    mixed = lax.psum_scatter(
        jnp.dot(rows, full_weight, preferred_element_type=jnp.float32).astype(jnp.bfloat16),
        "tensor",
        scatter_dimension=0,
        tiled=True,
    )
    grad_attended = lax.dot_general(
        lax.all_gather(grad_out, "tensor", axis=0, tiled=True),
        full_weight,
        (((1,), (1,)), ((), ())),
        preferred_element_type=jnp.float32,
    )
    grad_low = grad_attended.astype(jnp.bfloat16)
    routed_grad = lax.all_to_all(
        to_buffer(grad_low), "seq", split_axis=0, concat_axis=0, tiled=True
    )
    grad_cells = to_cells(routed_grad)
    backward_low = probs.astype(jnp.bfloat16)
    delta = jnp.einsum(
        "hcqd,hcqd->hcq", grad_cells, attended_cells, preferred_element_type=jnp.float32
    )
    grad_value = jnp.einsum(
        "hcqk,hcqd->hckd", backward_low, grad_cells, preferred_element_type=jnp.float32
    ).astype(jnp.bfloat16)
    grad_probs = jnp.einsum(
        "hcqd,hckd->hcqk", grad_cells, value_cells, preferred_element_type=jnp.float32
    )
    grad_scores = (probs * (grad_probs - delta[..., None])).astype(jnp.bfloat16)
    grad_query = (
        jnp.einsum("hcqk,hckd->hcqd", grad_scores, key_cells, preferred_element_type=jnp.float32)
        * score_scale
    ).astype(jnp.bfloat16)
    grad_key = (
        jnp.einsum("hcqk,hcqd->hckd", grad_scores, query_cells, preferred_element_type=jnp.float32)
        * score_scale
    ).astype(jnp.bfloat16)
    back_query, back_key, back_value = (
        lax.all_to_all(to_returns(grad_query), "seq", split_axis=0, concat_axis=0, tiled=True),
        lax.all_to_all(to_returns(grad_key), "seq", split_axis=0, concat_axis=0, tiled=True),
        lax.all_to_all(to_returns(grad_value), "seq", split_axis=0, concat_axis=0, tiled=True),
    )
    return (mixed, from_buffer(back_query), from_buffer(back_key), from_buffer(back_value))


def solution(mesh):
    return jax.shard_map(
        shards,
        mesh=mesh,
        in_specs=(
            P("seq", "tensor"),
            P("seq", "tensor"),
            P("seq", "tensor"),
            P("tensor", "seq"),
            P("tensor", "seq"),
            P("tensor", "seq"),
            P(("seq", "tensor"), None),
        ),
        out_specs=(
            P(("seq", "tensor"), None),
            P("seq", "tensor"),
            P("seq", "tensor"),
            P("seq", "tensor"),
        ),
        check_vma=False,
    )
```

profile of v0, /device:TPU:1, one launch (start us, length us, event | category | flops | bytes accessed | tf_op | source)
XLA Modules:
  0.0 222.1 jit_solution(9738105872773169787)
XLA Ops:
  9.9 11.7 %all-to-all-start = ((s32[64,4,4]{1,2,0:T(4,128)}), s32[64,4,4]{1,2,0:T(4,128)S(1)}, u32[]{:S(2)}, u32[]{:S(2)}) async-start(s32[64,4,4]{1,2,0:T(4,128)} %copy.55), calls=%async_computation | async-start | bytes 262144 | tf_op jit(solution)/shard_map/all_to_all | solution.py:55
  22.9 9.8 %all-to-all-done = s32[64,4,4]{1,2,0:T(4,128)S(1)} async-done(((s32[64,4,4]{1,2,0:T(4,128)}), s32[64,4,4]{1,2,0:T(4,128)S(1)}, u32[]{:S(2)}, u32[]{:S(2)}) %all-to-all-start) | async-done | bytes 4128 | tf_op jit(solution)/shard_map/all_to_all | solution.py:55
  32.8 4.4 %all-to-all-start.2 = ((bf16[64,4,512]{2,1,0:T(4,128)(2,1)}), bf16[64,4,512]{2,1,0:T(4,128)(2,1)S(1)}, u32[]{:S(2)}, u32[]{:S(2)}) async-start(bf16[64,4,512]{2,1,0:T(4,128)(2,1)} %all_to_all.61), calls=%async_computation.2 | async-start | bytes 524288 | tf_op jit(solution)/shard_map/all_to_all | solution.py:58
  38.5 12.2 %all-to-all-done.2 = bf16[64,4,512]{2,1,0:T(4,128)(2,1)S(1)} async-done(((bf16[64,4,512]{2,1,0:T(4,128)(2,1)}), bf16[64,4,512]{2,1,0:T(4,128)(2,1)S(1)}, u32[]{:S(2)}, u32[]{:S(2)}) %all-to-all-start.2) | async-done | bytes 262176 | tf_op jit(solution)/shard_map/all_to_all | solution.py:58
  50.8 4.8 %all-to-all-start.1 = ((bf16[64,4,512]{2,1,0:T(4,128)(2,1)}), bf16[64,4,512]{2,1,0:T(4,128)(2,1)S(1)}, u32[]{:S(2)}, u32[]{:S(2)}) async-start(bf16[64,4,512]{2,1,0:T(4,128)(2,1)} %all_to_all.59), calls=%async_computation.1 | async-start | bytes 524288 | tf_op jit(solution)/shard_map/all_to_all | solution.py:57
  56.8 11.8 %all-to-all-done.1 = bf16[64,4,512]{2,1,0:T(4,128)(2,1)S(1)} async-done(((bf16[64,4,512]{2,1,0:T(4,128)(2,1)}), bf16[64,4,512]{2,1,0:T(4,128)(2,1)S(1)}, u32[]{:S(2)}, u32[]{:S(2)}) %all-to-all-start.1) | async-done | bytes 262176 | tf_op jit(solution)/shard_map/all_to_all | solution.py:57
  68.6 4.8 %all-to-all-start.3 = ((bf16[64,4,512]{2,1,0:T(4,128)(2,1)}), bf16[64,4,512]{2,1,0:T(4,128)(2,1)S(1)}, u32[]{:S(2)}, u32[]{:S(2)}) async-start(bf16[64,4,512]{2,1,0:T(4,128)(2,1)} %all_to_all.63), calls=%async_computation.3 | async-start | bytes 524288 | tf_op jit(solution)/shard_map/all_to_all | solution.py:59
  73.4 27.2 %all_gather.7 = bf16[128,2048]{1,0:T(8,128)(2,1)S(1)} all-gather(bf16[16,2048]{1,0:T(8,128)(2,1)S(1)} %copy-done.2), channel_id=1, replica_groups=mesh['seq'=64,'tensor'=8] {'tensor'}, dimensions={0}, use_global_device_ids=true | all-gather | bytes 589824 | tf_op jit(solution)/shard_map/all_gather | solution.py:107
  102.1 2.0 convolution_convert_fusion.18
  105.6 15.0 %all-to-all-start.5 = ((bf16[64,4,512]{2,1,0:T(4,128)(2,1)}), bf16[64,4,512]{2,1,0:T(4,128)(2,1)S(1)}, u32[]{:S(2)}, u32[]{:S(2)}) async-start(bf16[64,4,512]{2,1,0:T(4,128)(2,1)} %all_to_all.67), calls=%async_computation.6 | async-start | bytes 524288 | tf_op jit(solution)/shard_map/all_to_all | solution.py:113
  121.1 1.3 fusion.66
  122.4 11.2 %all-to-all-done.5 = bf16[64,4,512]{2,1,0:T(4,128)(2,1)S(1)} async-done(((bf16[64,4,512]{2,1,0:T(4,128)(2,1)}), bf16[64,4,512]{2,1,0:T(4,128)(2,1)S(1)}, u32[]{:S(2)}, u32[]{:S(2)}) %all-to-all-start.5) | async-done | bytes 262176 | tf_op jit(solution)/shard_map/all_to_all | solution.py:113
  135.8 4.8 %all-to-all-start.4 = ((bf16[64,4,512]{2,1,0:T(4,128)(2,1)}), bf16[64,4,512]{2,1,0:T(4,128)(2,1)S(1)}, u32[]{:S(2)}, u32[]{:S(2)}) async-start(bf16[64,4,512]{2,1,0:T(4,128)(2,1)} %all_to_all.65), calls=%async_computation.4 | async-start | bytes 524288 | tf_op jit(solution)/shard_map/all_to_all | solution.py:94
  142.5 11.2 %all-to-all-done.4 = bf16[64,4,512]{2,1,0:T(4,128)(2,1)S(1)} async-done(((bf16[64,4,512]{2,1,0:T(4,128)(2,1)}), bf16[64,4,512]{2,1,0:T(4,128)(2,1)S(1)}, u32[]{:S(2)}, u32[]{:S(2)}) %all-to-all-start.4) | async-done | bytes 262176 | tf_op jit(solution)/shard_map/all_to_all | solution.py:94
  153.7 4.8 %all-to-all-start.8 = ((bf16[64,4,512]{2,1,0:T(4,128)(2,1)}), bf16[64,4,512]{2,1,0:T(4,128)(2,1)S(1)}, u32[]{:S(2)}, u32[]{:S(2)}) async-start(bf16[64,4,512]{2,1,0:T(4,128)(2,1)} %all_to_all.73), calls=%async_computation.9 | async-start | bytes 524288 | tf_op jit(solution)/shard_map/all_to_all | solution.py:139
  158.7 1.1 fusion.10
  159.7 1.1 copy.79
  162.1 9.5 %all-to-all-done.8 = bf16[64,4,512]{2,1,0:T(4,128)(2,1)S(1)} async-done(((bf16[64,4,512]{2,1,0:T(4,128)(2,1)}), bf16[64,4,512]{2,1,0:T(4,128)(2,1)S(1)}, u32[]{:S(2)}, u32[]{:S(2)}) %all-to-all-start.8) | async-done | bytes 262176 | tf_op jit(solution)/shard_map/all_to_all | solution.py:139
  171.5 4.8 %all-to-all-start.7 = ((bf16[64,4,512]{2,1,0:T(4,128)(2,1)}), bf16[64,4,512]{2,1,0:T(4,128)(2,1)S(1)}, u32[]{:S(2)}, u32[]{:S(2)}) async-start(bf16[64,4,512]{2,1,0:T(4,128)(2,1)} %all_to_all.71), calls=%async_computation.8 | async-start | bytes 524288 | tf_op jit(solution)/shard_map/all_to_all | solution.py:138
  176.4 1.6 convolution_convert_fusion
  179.7 9.7 %all-to-all-done.7 = bf16[64,4,512]{2,1,0:T(4,128)(2,1)S(1)} async-done(((bf16[64,4,512]{2,1,0:T(4,128)(2,1)}), bf16[64,4,512]{2,1,0:T(4,128)(2,1)S(1)}, u32[]{:S(2)}, u32[]{:S(2)}) %all-to-all-start.7) | async-done | bytes 262176 | tf_op jit(solution)/shard_map/all_to_all | solution.py:138
  189.4 4.8 %all-to-all-start.6 = ((bf16[64,4,512]{2,1,0:T(4,128)(2,1)}), bf16[64,4,512]{2,1,0:T(4,128)(2,1)S(1)}, u32[]{:S(2)}, u32[]{:S(2)}) async-start(bf16[64,4,512]{2,1,0:T(4,128)(2,1)} %all_to_all.69), calls=%async_computation.7 | async-start | bytes 524288 | tf_op jit(solution)/shard_map/all_to_all | solution.py:137
  196.5 10.8 %all-to-all-done.6 = bf16[64,4,512]{2,1,0:T(4,128)(2,1)S(1)} async-done(((bf16[64,4,512]{2,1,0:T(4,128)(2,1)}), bf16[64,4,512]{2,1,0:T(4,128)(2,1)S(1)}, u32[]{:S(2)}, u32[]{:S(2)}) %all-to-all-start.6) | async-done | bytes 262176 | tf_op jit(solution)/shard_map/all_to_all | solution.py:137
  208.4 6.8 %reduce-scatter.2.cloned.1.call-done = bf16[16,2048]{1,0:T(8,128)(2,1)} async-done(((bf16[128,2048]{1,0:T(8,128)(2,1)}), bf16[16,2048]{1,0:T(8,128)(2,1)}) %reduce-scatter.2.cloned.1.call-update) | async-done | bytes 65552 | tf_op jit(solution)/shard_map/reduce_scatter | solution.py:100
  (76 shorter events, 20.4 us)
Async XLA Ops:
  7.2 14.5 %copy-start = (bf16[128,512]{1,0:T(8,128)(2,1)S(1)}, bf16[128,512]{1,0:T(8,128)(2,1)}, u32[]{:S(2)}) copy-start(bf16[128,512]{1,0:T(8,128)(2,1)} %param.8) | copy-start | bytes 393220
  7.2 30.1 %copy-start.3 = (bf16[128,512]{1,0:T(8,128)(2,1)S(1)}, bf16[128,512]{1,0:T(8,128)(2,1)}, u32[]{:S(2)}) copy-start(bf16[128,512]{1,0:T(8,128)(2,1)} %param.7) | copy-start | bytes 393220
  7.2 94.9 %all-gather.2.cloned.1.call-start = ((), (), s32[]{:S(2)}) async-start(), calls=%async_computation.10 | async-start | bytes 2129920 | tf_op jit(solution)/shard_map/all_gather | solution.py:98
  9.9 45.6 %copy-start.4 = (bf16[128,512]{1,0:T(8,128)(2,1)S(1)}, bf16[128,512]{1,0:T(8,128)(2,1)}, u32[]{:S(2)}) copy-start(bf16[128,512]{1,0:T(8,128)(2,1)} %param.9) | copy-start | bytes 393220
  9.9 22.8 %all-to-all-start = ((s32[64,4,4]{1,2,0:T(4,128)}), s32[64,4,4]{1,2,0:T(4,128)S(1)}, u32[]{:S(2)}, u32[]{:S(2)}) async-start(s32[64,4,4]{1,2,0:T(4,128)} %copy.55), calls=%async_computation | async-start | bytes 262144 | tf_op jit(solution)/shard_map/all_to_all | solution.py:55
  32.8 18.0 %all-to-all-start.2 = ((bf16[64,4,512]{2,1,0:T(4,128)(2,1)}), bf16[64,4,512]{2,1,0:T(4,128)(2,1)S(1)}, u32[]{:S(2)}, u32[]{:S(2)}) async-start(bf16[64,4,512]{2,1,0:T(4,128)(2,1)} %all_to_all.61), calls=%async_computation.2 | async-start | bytes 524288 | tf_op jit(solution)/shard_map/all_to_all | solution.py:58
  37.3 36.2 %copy-start.2 = (bf16[16,2048]{1,0:T(8,128)(2,1)S(1)}, bf16[16,2048]{1,0:T(8,128)(2,1)}, u32[]{:S(2)}) copy-start(bf16[16,2048]{1,0:T(8,128)(2,1)} %param.13) | copy-start | bytes 196612
  50.8 17.9 %all-to-all-start.1 = ((bf16[64,4,512]{2,1,0:T(4,128)(2,1)}), bf16[64,4,512]{2,1,0:T(4,128)(2,1)S(1)}, u32[]{:S(2)}, u32[]{:S(2)}) async-start(bf16[64,4,512]{2,1,0:T(4,128)(2,1)} %all_to_all.59), calls=%async_computation.1 | async-start | bytes 524288 | tf_op jit(solution)/shard_map/all_to_all | solution.py:57
  68.6 32.7 %all-to-all-start.3 = ((bf16[64,4,512]{2,1,0:T(4,128)(2,1)}), bf16[64,4,512]{2,1,0:T(4,128)(2,1)S(1)}, u32[]{:S(2)}, u32[]{:S(2)}) async-start(bf16[64,4,512]{2,1,0:T(4,128)(2,1)} %all_to_all.63), calls=%async_computation.3 | async-start | bytes 524288 | tf_op jit(solution)/shard_map/all_to_all | solution.py:59
  105.6 28.0 %all-to-all-start.5 = ((bf16[64,4,512]{2,1,0:T(4,128)(2,1)}), bf16[64,4,512]{2,1,0:T(4,128)(2,1)S(1)}, u32[]{:S(2)}, u32[]{:S(2)}) async-start(bf16[64,4,512]{2,1,0:T(4,128)(2,1)} %all_to_all.67), calls=%async_computation.6 | async-start | bytes 524288 | tf_op jit(solution)/shard_map/all_to_all | solution.py:113
  135.8 17.9 %all-to-all-start.4 = ((bf16[64,4,512]{2,1,0:T(4,128)(2,1)}), bf16[64,4,512]{2,1,0:T(4,128)(2,1)S(1)}, u32[]{:S(2)}, u32[]{:S(2)}) async-start(bf16[64,4,512]{2,1,0:T(4,128)(2,1)} %all_to_all.65), calls=%async_computation.4 | async-start | bytes 524288 | tf_op jit(solution)/shard_map/all_to_all | solution.py:94
  153.7 17.9 %all-to-all-start.8 = ((bf16[64,4,512]{2,1,0:T(4,128)(2,1)}), bf16[64,4,512]{2,1,0:T(4,128)(2,1)S(1)}, u32[]{:S(2)}, u32[]{:S(2)}) async-start(bf16[64,4,512]{2,1,0:T(4,128)(2,1)} %all_to_all.73), calls=%async_computation.9 | async-start | bytes 524288 | tf_op jit(solution)/shard_map/all_to_all | solution.py:139
  158.4 17.9 %copy-start.1 = (bf16[512,2048]{0,1:T(8,128)(2,1)S(1)}, bf16[512,2048]{0,1:T(8,128)(2,1)}, u32[]{:S(2)}) copy-start(bf16[512,2048]{0,1:T(8,128)(2,1)} %all-gather.2.cloned.1.call-done) | copy-start | bytes 6291460
  171.5 17.9 %all-to-all-start.7 = ((bf16[64,4,512]{2,1,0:T(4,128)(2,1)}), bf16[64,4,512]{2,1,0:T(4,128)(2,1)S(1)}, u32[]{:S(2)}, u32[]{:S(2)}) async-start(bf16[64,4,512]{2,1,0:T(4,128)(2,1)} %all_to_all.71), calls=%async_computation.8 | async-start | bytes 524288 | tf_op jit(solution)/shard_map/all_to_all | solution.py:138
  176.3 38.9 %reduce-scatter.2.cloned.1.call-start = ((), (), s32[]{:S(2)}) async-start(), calls=%async_computation.11 | async-start | bytes 589824 | tf_op jit(solution)/shard_map/reduce_scatter | solution.py:100
  189.4 17.9 %all-to-all-start.6 = ((bf16[64,4,512]{2,1,0:T(4,128)(2,1)}), bf16[64,4,512]{2,1,0:T(4,128)(2,1)S(1)}, u32[]{:S(2)}, u32[]{:S(2)}) async-start(bf16[64,4,512]{2,1,0:T(4,128)(2,1)} %all_to_all.69), calls=%async_computation.7 | async-start | bytes 524288 | tf_op jit(solution)/shard_map/all_to_all | solution.py:137
Sparse Core Ops, SparseCore 0:
  11.3 89.4 all-gather.1
  180.5 34.6 reduce-scatter.1
where the time goes:
time: 226 us; the launch traced here: 222 us
  waiting for transfers between devices  93.8 us (42%)
  starting transfers between devices  59.9 us (27%)
  blocking collectives  27.2 us (12%)
  between operations  14.5 us (6%)
  local copies, waits for them, and re-layouts  13.3 us (6%)
  matrix products  11.1 us (5%)
    all_gather x1, blocking collectives, shards(): lax.all_gather(grad_out, 'tensor', axis=0, tiled=True)  27.2 us
    all_to_all x1, starting transfers between devices, shards(): lax.all_to_all(to_buffer(grad_low), 'seq', split_axis=0, concat_axis=0, t...  15 us
    all_to_all x1, waiting for transfers between devices, shards(): lax.all_to_all(to_buffer(key_rows), 'seq', split_axis=0, concat_axis=0, t...  12.2 us
    all_to_all x1, waiting for transfers between devices, shards(): lax.all_to_all(to_buffer(query_rows), 'seq', split_axis=0, concat_axis=0,...  11.8 us
    all_to_all x1, starting transfers between devices, shards(): lax.all_to_all(target_rows, 'seq', split_axis=0, concat_axis=0, tiled=True)  11.7 us
    all_to_all x1, waiting for transfers between devices, shards(): lax.all_to_all(to_returns(attended_cells), 'seq', split_axis=0, concat_ax...  11.2 us
    all_to_all x1, waiting for transfers between devices, shards(): lax.all_to_all(to_buffer(grad_low), 'seq', split_axis=0, concat_axis=0, t...  11.2 us
    all_to_all x1, waiting for transfers between devices, shards(): lax.all_to_all(to_returns(grad_query), 'seq', split_axis=0, concat_axis=0...  10.8 us
  transfers between devices with their start and end apart: 11, of which 9 were waited for; matrix products, arithmetic and copies ran while one was open for 7% of the time, Pallas kernels for 0%

commit v1 on v0

v1 whole, which is shorter than its diff:
```python
import functools
import math

import jax
import jax.numpy as jnp
from jax import lax
from jax.experimental import pallas as pl
from jax.experimental.pallas import tpu as pltpu
from jax.sharding import PartitionSpec as P

CLU_DEV = 8
SLOTS = 4
MESH = pl.DeviceIdType.MESH
F32 = jnp.float32
BF16 = jnp.bfloat16
NN = (((1,), (0,)), ((), ()))
NT = (((1,), (1,)), ((), ()))
TN = (((0,), (0,)), ((), ()))


def dot(a, b, dims=NN):
    return lax.dot_general(a, b, dims, preferred_element_type=F32)


def iota(shape, dim):
    return lax.broadcasted_iota(jnp.int32, shape, dim)


def kernel(
    dims,
    q_ref,
    k_ref,
    v_ref,
    cid_ref,
    w_ref,
    go_ref,
    mixed_ref,
    dq_ref,
    dk_ref,
    dv_ref,
    xcat,
    pack,
    unpack,
    msnd,
    mrcv,
    snd1,
    rcv1,
    sndg,
    rcvg,
    snda,
    rcva,
    sndb,
    rcvb,
    wt,
    gout,
    rsnd,
    rrcv,
    cells,
    probs,
    outs,
    ssem,
    rsem,
):
    ny, nx, nt, heads, tok, dh = dims
    ns = ny * nx * 2
    blk = heads * SLOTS
    peers = min(16, ns)
    chunks = ns // peers
    rows = peers * blk
    part = peers * SLOTS
    recv_rows = ns * SLOTS
    scale = 1.0 / math.sqrt(dh)
    me = lax.axis_index("seq")
    mt = lax.axis_index("tensor")
    my = lax.div(me, 2 * nx)
    mx = lax.rem(lax.div(me, 2), nx)
    mc = lax.rem(me, 2)

    barrier = pltpu.get_barrier_semaphore()

    def greet_seq(j, carry):
        pl.semaphore_signal(
            barrier, inc=1, device_id={"seq": lax.rem(me + j, ns)}, device_id_type=MESH
        )
        return carry

    lax.fori_loop(1, ns, greet_seq, 0)

    def greet_tensor(j, carry):
        pl.semaphore_signal(
            barrier, inc=1, device_id={"tensor": lax.rem(mt + j, nt)}, device_id_type=MESH
        )
        return carry

    lax.fori_loop(1, nt, greet_tensor, 0)

    def remote(src, dst, index, target):
        return pltpu.make_async_remote_copy(
            src_ref=src,
            dst_ref=dst,
            send_sem=ssem.at[index],
            recv_sem=rsem.at[index],
            device_id=target,
            device_id_type=MESH,
        )

    def wait_recv(ref, index):
        pltpu.make_async_copy(ref, ref, rsem.at[index]).wait()

    def wait_send(ref, index):
        pltpu.make_async_copy(ref, ref, ssem.at[index]).wait()

    def exchange(src, dst, index):
        def step(j, carry):
            ahead = lax.rem(me + j, ns)
            behind = lax.rem(me + ns - j, ns)
            remote(src.at[ahead], dst.at[me], index, {"seq": ahead}).start()
            remote(src.at[behind], dst.at[me], index, {"seq": behind}).start()
            return carry

        lax.fori_loop(1, ns // 2, step, 0)
        far = lax.rem(me + ns // 2, ns)
        remote(src.at[far], dst.at[me], index, {"seq": far}).start()

    wt[my, mx, mc] = dot(
        (iota((32, 32), 0) == iota((32, 32), 1)).astype(BF16), w_ref[...], NT
    ).astype(BF16)
    gout[mt] = go_ref[...]

    upper = (iota((tok, tok), 0) < iota((tok, tok), 1)).astype(BF16)
    diag = iota((tok, tok), 0) == iota((tok, tok), 1)
    table = jnp.zeros((ns, 128), F32)
    for h in range(heads):
        cid = cid_ref[h : h + 1, :]
        owner = lax.shift_right_logical(cid, 3)
        member = iota((ns, tok), 0) == owner
        onehot = member.astype(F32)
        earlier = dot(onehot.astype(BF16), upper)
        rank = jnp.sum(onehot * earlier, axis=0, keepdims=True).astype(jnp.int32)
        dest = owner * blk + h * SLOTS + rank
        for c in range(chunks):
            pack[c, :, h * tok : (h + 1) * tok] = (
                iota((rows, tok), 0) + c * rows == dest
            ).astype(BF16)
        column = jnp.sum(jnp.where(diag, dest, 0).astype(F32), axis=1, keepdims=True).astype(
            jnp.int32
        )
        unpack[h] = (iota((tok, ns * blk), 1) == column).astype(BF16)
        value = jnp.where(member, (cid & (CLU_DEV - 1)) + 1, 0).astype(F32).astype(BF16)
        lane = (iota((128, tok), 0) == rank + h * SLOTS).astype(BF16)
        table = table + dot(value, lane, NT)
        for t, ref in enumerate((q_ref, k_ref, v_ref)):
            xcat[h * tok : (h + 1) * tok, t * dh : (t + 1) * dh] = ref[:, h * dh : (h + 1) * dh]
    msnd[...] = table.reshape(ns, 1, 128)

    def pack_rows(c, carry):
        packed = dot(pack[c], xcat[...]).astype(BF16)
        for t in range(3):
            snd1[pl.ds(c * peers, peers), t] = packed[:, t * dh : (t + 1) * dh].reshape(
                peers, blk, dh
            )
        return carry

    lax.fori_loop(0, chunks, pack_rows, 0)

    pl.semaphore_wait(barrier, ns - 1 + nt - 1)

    def weight_y(j, carry):
        target = (lax.rem(my + j, ny) * nx + mx) * 2 + mc
        remote(wt.at[my, mx, mc], wt.at[my, mx, mc], 0, {"seq": target}).start()
        return carry

    lax.fori_loop(1, ny, weight_y, 0)

    def cotangent(j, carry):
        remote(gout.at[mt], gout.at[mt], 3, {"tensor": lax.rem(mt + j, nt)}).start()
        return carry

    lax.fori_loop(1, nt, cotangent, 0)

    exchange(msnd, mrcv, 4)
    exchange(snd1, rcv1, 5)
    mrcv[me] = msnd[me]
    rcv1[me] = snd1[me]

    wait_recv(wt.at[pl.ds(0, ny - 1), 0, 0], 0)

    def weight_x(j, carry):
        target = (my * nx + lax.rem(mx + j, nx)) * 2 + mc
        remote(wt.at[:, mx, mc], wt.at[:, mx, mc], 1, {"seq": target}).start()
        return carry

    lax.fori_loop(1, nx, weight_x, 0)
    wait_recv(wt.at[:, pl.ds(0, nx - 1), 0], 1)
    other = me + 1 - 2 * mc
    remote(wt.at[:, :, mc], wt.at[:, :, mc], 2, {"seq": other}).start()
    wait_recv(wt.at[:, :, 0], 2)
    wait_recv(gout.at[pl.ds(0, nt - 1)], 3)

    columns = nx * 2 * 32
    grad = jnp.zeros((tok, heads * dh), F32)
    for y in range(ny):
        grad = grad + dot(
            gout[:, :, y * columns : (y + 1) * columns].reshape(tok, columns),
            wt[y].reshape(columns, heads * dh),
        )
    grad = grad.astype(BF16)
    for h in range(heads):
        xcat[h * tok : (h + 1) * tok, :dh] = grad[:, h * dh : (h + 1) * dh]

    def pack_grad(c, carry):
        sndg[pl.ds(c * peers, peers)] = (
            dot(pack[c], xcat[:, :dh]).astype(BF16).reshape(peers, blk, dh)
        )
        return carry

    lax.fori_loop(0, chunks, pack_grad, 0)
    exchange(sndg, rcvg, 6)
    rcvg[me] = sndg[me]

    def source(index):
        h = lax.div(index, part)
        rest = index - h * part
        p = lax.div(rest, SLOTS)
        return p * blk + h * SLOTS + (rest - p * SLOTS)

    to_heads = (source(iota((rows, 1), 0)) == iota((rows, rows), 1)).astype(BF16)
    to_peers = (source(iota((1, rows), 1)) == iota((rows, rows), 0)).astype(BF16)

    wait_recv(mrcv.at[pl.ds(0, ns - 1)], 4)
    wait_recv(rcv1.at[pl.ds(0, ns - 1)], 5)

    lanes = iota((rows, 128), 1)
    own_lane = lanes == (iota((rows, 128), 0) & (blk - 1))

    def by_head(c, index, values):
        moved = dot(to_heads, values).astype(BF16)
        for h in range(heads):
            cells[index, h, c] = moved[h * part : (h + 1) * part]

    def split_heads(c, carry):
        spread = jnp.broadcast_to(
            mrcv[pl.ds(c * peers, peers)], (peers, blk, 128)
        ).reshape(rows, 128)
        mark = jnp.sum(jnp.where(own_lane, spread, 0.0), axis=1, keepdims=True)
        marks = ((lanes.astype(F32) == mark) & (lanes > 0)).astype(BF16)
        by_head(c, 0, marks)
        for t in range(3):
            by_head(c, 1 + t, rcv1[pl.ds(c * peers, peers), t].reshape(rows, dh))
        return carry

    lax.fori_loop(0, chunks, split_heads, 0)

    def cell(index, h):
        return cells[index, h].reshape(recv_rows, dh)

    def forward(h, carry):
        marks = cell(0, h)
        same = dot(marks, marks, NT) > 0.5
        scores = jnp.where(same, dot(cell(1, h), cell(2, h), NT) * scale, -1e30)
        weights = jnp.exp(scores - jnp.max(scores, axis=1, keepdims=True))
        prob = weights / jnp.sum(weights, axis=1, keepdims=True)
        probs[h] = prob
        outs[0, h] = (
            dot(prob.astype(BF16), cell(3, h)).astype(BF16).reshape(chunks, part, dh)
        )
        return carry

    lax.fori_loop(0, heads, forward, 0)

    def by_peer(c, index):
        return (
            dot(to_peers, outs[index, :, c].reshape(rows, dh))
            .astype(BF16)
            .reshape(peers, blk, dh)
        )

    def return_attended(c, carry):
        snda[pl.ds(c * peers, peers)] = by_peer(c, 0)
        return carry

    lax.fori_loop(0, chunks, return_attended, 0)
    exchange(snda, rcva, 7)
    rcva[me] = snda[me]

    wait_recv(rcvg.at[pl.ds(0, ns - 1)], 6)

    def split_grad(c, carry):
        by_head(c, 4, rcvg[pl.ds(c * peers, peers)].reshape(rows, dh))
        return carry

    lax.fori_loop(0, chunks, split_grad, 0)

    def backward(h, carry):
        grads = cell(4, h)
        prob = probs[h]
        attended = outs[0, h].reshape(recv_rows, dh)
        delta = jnp.sum(grads.astype(F32) * attended.astype(F32), axis=1, keepdims=True)
        grad_value = dot(prob.astype(BF16), grads, TN)
        grad_probs = dot(grads, cell(3, h), NT)
        grad_scores = (prob * (grad_probs - delta)).astype(BF16)
        grad_query = dot(grad_scores, cell(2, h)) * scale
        grad_key = dot(grad_scores, cell(1, h), TN) * scale
        for t, value in enumerate((grad_query, grad_key, grad_value)):
            outs[1 + t, h] = value.astype(BF16).reshape(chunks, part, dh)
        return carry

    lax.fori_loop(0, heads, backward, 0)

    def return_grads(c, carry):
        for t in range(3):
            sndb[pl.ds(c * peers, peers), t] = by_peer(c, 1 + t)
        return carry

    lax.fori_loop(0, chunks, return_grads, 0)
    exchange(sndb, rcvb, 8)
    rcvb[me] = sndb[me]

    wait_recv(rcva.at[pl.ds(0, ns - 1)], 7)
    arrived = rcva[...].reshape(ns * blk, dh)
    attended = jnp.concatenate(
        [dot(unpack[h], arrived).astype(BF16) for h in range(heads)], axis=1
    )

    def project(y, carry):
        rsnd[:, y] = (
            dot(attended, wt[y].reshape(columns, heads * dh), NT)
            .astype(BF16)
            .reshape(nt, tok // nt, columns)
        )
        return carry

    lax.fori_loop(0, ny, project, 0)

    def scatter(j, carry):
        target = lax.rem(mt + j, nt)
        remote(rsnd.at[target], rrcv.at[mt], 9, {"tensor": target}).start()
        return carry

    lax.fori_loop(1, nt, scatter, 0)
    rrcv[mt] = rsnd[mt]
    wait_recv(rrcv.at[pl.ds(0, nt - 1)], 9)
    for y in range(ny):
        total = rrcv[0, y].astype(F32)
        for t in range(1, nt):
            total = total + rrcv[t, y].astype(F32)
        mixed_ref[:, y * columns : (y + 1) * columns] = total.astype(BF16)

    wait_recv(rcvb.at[pl.ds(0, ns - 1)], 8)
    for t, ref in enumerate((dq_ref, dk_ref, dv_ref)):
        back = rcvb[:, t].reshape(ns * blk, dh)
        for h in range(heads):
            ref[:, h * dh : (h + 1) * dh] = dot(unpack[h], back).astype(BF16)

    wait_send(wt.at[pl.ds(0, ny - 1), 0, 0], 0)
    wait_send(wt.at[:, pl.ds(0, nx - 1), 0], 1)
    wait_send(wt.at[:, :, 0], 2)
    wait_send(gout.at[pl.ds(0, nt - 1)], 3)
    wait_send(msnd.at[pl.ds(0, ns - 1)], 4)
    wait_send(snd1.at[pl.ds(0, ns - 1)], 5)
    wait_send(sndg.at[pl.ds(0, ns - 1)], 6)
    wait_send(snda.at[pl.ds(0, ns - 1)], 7)
    wait_send(sndb.at[pl.ds(0, ns - 1)], 8)
    wait_send(rsnd.at[pl.ds(0, nt - 1)], 9)


def solution(mesh, grid=(8, 4)):
    ny, nx = grid
    ns, nt = mesh.shape["seq"], mesh.shape["tensor"]

    def shards(query_rows, key_rows, value_rows, cluster_id, slot_index, out_weight, grad_out):
        tok = query_rows.shape[0]
        heads = cluster_id.shape[0]
        dh = query_rows.shape[1] // heads
        blk = heads * SLOTS
        peers = min(16, ns)
        chunks = ns // peers
        rows = peers * blk
        part = peers * SLOTS
        columns = nx * 2 * 32
        vmem = pl.BlockSpec(memory_space=pltpu.VMEM)
        wide = jax.ShapeDtypeStruct(query_rows.shape, BF16)
        one = pltpu.VMEM((ns, blk, dh), BF16)
        three = pltpu.VMEM((ns, 3, blk, dh), BF16)
        return pl.pallas_call(
            functools.partial(kernel, (ny, nx, nt, heads, tok, dh)),
            out_shape=(jax.ShapeDtypeStruct(grad_out.shape, BF16), wide, wide, wide),
            in_specs=[vmem] * 6,
            out_specs=(vmem,) * 4,
            scratch_shapes=[
                pltpu.VMEM((heads * tok, 3 * dh), BF16),
                pltpu.VMEM((chunks, rows, heads * tok), BF16),
                pltpu.VMEM((heads, tok, ns * blk), BF16),
                pltpu.VMEM((ns, 1, 128), F32),
                pltpu.VMEM((ns, 1, 128), F32),
                three,
                three,
                one,
                one,
                one,
                one,
                three,
                three,
                pltpu.VMEM((ny, nx, 2, 32, heads * dh), BF16),
                pltpu.VMEM((nt,) + grad_out.shape, BF16),
                pltpu.VMEM((nt, ny, tok // nt, columns), BF16),
                pltpu.VMEM((nt, ny, tok // nt, columns), BF16),
                pltpu.VMEM((5, heads, chunks, part, dh), BF16),
                pltpu.VMEM((heads, ns * SLOTS, ns * SLOTS), F32),
                pltpu.VMEM((4, heads, chunks, part, dh), BF16),
                pltpu.SemaphoreType.DMA((10,)),
                pltpu.SemaphoreType.DMA((10,)),
            ],
            compiler_params=pltpu.CompilerParams(
                collective_id=0, has_side_effects=True, vmem_limit_bytes=48 * 1024 * 1024
            ),
        )(query_rows, key_rows, value_rows, cluster_id, out_weight, grad_out)

    return jax.shard_map(
        shards,
        mesh=mesh,
        in_specs=(
            P("seq", "tensor"),
            P("seq", "tensor"),
            P("seq", "tensor"),
            P("tensor", "seq"),
            P("tensor", "seq"),
            P("tensor", "seq"),
            P(("seq", "tensor"), None),
        ),
        out_specs=(
            P(("seq", "tensor"), None),
            P("seq", "tensor"),
            P("seq", "tensor"),
            P("seq", "tensor"),
        ),
        check_vma=False,
    )
```

time: 226 us -> 88 us (0.39); the launches traced: 222 us -> 87.4 us
  waiting for transfers between devices: 93.8 us -> 0 us
  Pallas kernels: 0 us -> 80.5 us
  starting transfers between devices: 59.9 us -> 0 us
  blocking collectives: 27.2 us -> 0 us
  between operations: 14.5 us -> 0.69 us
  matrix products: 11.1 us -> 0 us
  local copies, waits for them, and re-layouts: 13.3 us -> 6.16 us
    all_to_all x9 -> x0, waiting for transfers between devices: 86.3 us -> none  [the longest x1 12.2 us: shards(): lax.all_to_all(to_buffer(key_rows), 'seq', split_axis=0, concat_axis=0, t...]
    pallas_call x0 -> x1, Pallas kernels: none -> 80.5 us  [shards(): pl.pallas_call(functools.partial(kernel, (ny, nx, nt, heads, tok, dh)), o...]
    all_to_all x9 -> x0, starting transfers between devices: 59.8 us -> none  [the longest x1 15 us: shards(): lax.all_to_all(to_buffer(grad_low), 'seq', split_axis=0, concat_axis=0, t...]
    all_gather x1 -> x0, blocking collectives: 27.2 us -> none  [shards(): lax.all_gather(grad_out, 'tensor', axis=0, tiled=True)]
    dot_general x26 -> x0, matrix products: 11.1 us -> none  [the longest x4 2.1 us: to_returns(): jnp.einsum('hrb,hrd->bhd', cell_table, flat, preferred_element_type=jnp.f...]
    all_to_all x12 -> x0, local copies, waits for them, and re-layouts: 7.47 us -> none  [the longest x4 1.02 us: shards(): lax.all_to_all(target_rows, 'seq', split_axis=0, concat_axis=0, tiled=True)]
    reduce_scatter x1 -> x0, waiting for transfers between devices: 6.83 us -> none  [shards(): lax.psum_scatter(jnp.dot(rows, full_weight, preferred_element_type=jnp.fl...]
    unnamed x13 -> x15, local copies, waits for them, and re-layouts: 2.34 us -> 6.16 us
  transfers between devices with their start and end apart: 11 -> 0, of which waited for: 9 -> 0; matrix products, arithmetic and copies ran while one was open for 7% -> 0% of each run, Pallas kernels for 0% -> 0%
where the time goes in v1:
time: 88 us; the launch traced here: 87.4 us
  Pallas kernels  80.5 us (91%)
  local copies, waits for them, and re-layouts  6.16 us (7%)
    pallas_call x1, Pallas kernels, shards(): pl.pallas_call(functools.partial(kernel, (ny, nx, nt, heads, tok, dh)), o...  80.5 us
    unnamed x15, local copies, waits for them, and re-layouts  6.16 us

profile of v1, /device:TPU:1, one launch (start us, length us, event | category | flops | bytes accessed | tf_op | source)
XLA Modules:
  0.0 87.4 jit_solution(10001912153920961273)
XLA Ops:
  0.6 0.0 copy-start.4
  0.6 0.0 copy-start
  0.7 0.9 %copy.10.w_ref = bf16[512,32]{1,0:T(8,128)(2,1)S(1)} copy(bf16[512,32]{0,1:T(8,128)(2,1)} %param.11) | data formatting | bytes 65536 | tf_op args[5]
  1.6 0.0 copy-done.4
  1.6 0.0 copy-done
  1.6 0.0 copy-start.1
  1.6 0.9 %copy-done.1 = bf16[128,512]{1,0:T(8,128)(2,1)S(1)} copy-done((bf16[128,512]{1,0:T(8,128)(2,1)S(1)}, bf16[128,512]{1,0:T(8,128)(2,1)}, u32[]{:S(2)}) %copy-start.1) | copy-done | bytes 131096
  2.5 0.0 copy-start.2
  2.5 0.9 %copy-done.2 = bf16[128,512]{1,0:T(8,128)(2,1)S(1)} copy-done((bf16[128,512]{1,0:T(8,128)(2,1)S(1)}, bf16[128,512]{1,0:T(8,128)(2,1)}, u32[]{:S(2)}) %copy-start.2) | copy-done | bytes 131096
  3.4 0.0 copy-start.3
  3.4 0.8 copy-done.3
  4.2 80.5 %shard_map.93 = (bf16[16,2048]{1,0:T(8,128)(2,1)S(1)}, bf16[128,512]{1,0:T(8,128)(2,1)S(1)}, bf16[128,512]{1,0:T(8,128)(2,1)S(1)}, bf16[128,512]{1,0:T(8,128)(2,1)S(1)}) custom-call(bf16[128,512]{1,0:T(8,128)(2,1)S(1)} %copy-done, bf16[128,512]{1,0:T(8,128)(2,1)S(1)} %copy-done.1, bf16[128,512]{1,0:T(8,128)(2,1)S(1)} %copy-done.2, s32[4,128]{1,0:T(4,128)S(1)} %copy-done.4, ...), custom_call_target="tpu_custom_call" | custom-call | tf_op jit(solution)/shard_map/pallas_call | solution.py:385
  84.8 0.6 copy.15
  85.4 0.7 copy.16
  86.1 0.7 copy.17
  86.7 0.7 copy.18
Async XLA Ops:
  0.6 0.9 %copy-start.4 = (s32[4,128]{1,0:T(4,128)S(1)}, s32[4,128]{1,0:T(4,128)}, u32[]{:S(2)}) copy-start(s32[4,128]{1,0:T(4,128)} %cid_ref.1) | copy-start | bytes 6148
  0.6 0.9 %copy-start = (bf16[128,512]{1,0:T(8,128)(2,1)S(1)}, bf16[128,512]{1,0:T(8,128)(2,1)}, u32[]{:S(2)}) copy-start(bf16[128,512]{1,0:T(8,128)(2,1)} %q_ref.1) | copy-start | bytes 393220
  1.6 0.9 %copy-start.1 = (bf16[128,512]{1,0:T(8,128)(2,1)S(1)}, bf16[128,512]{1,0:T(8,128)(2,1)}, u32[]{:S(2)}) copy-start(bf16[128,512]{1,0:T(8,128)(2,1)} %k_ref.1) | copy-start | bytes 393220
  2.5 0.9 %copy-start.2 = (bf16[128,512]{1,0:T(8,128)(2,1)S(1)}, bf16[128,512]{1,0:T(8,128)(2,1)}, u32[]{:S(2)}) copy-start(bf16[128,512]{1,0:T(8,128)(2,1)} %v_ref.1) | copy-start | bytes 393220
  3.4 0.8 copy-start.3

commit v2 on v1

v2 whole, which is shorter than its diff:
```python
import functools
import math

import jax
import jax.numpy as jnp
from jax import lax
from jax.experimental import pallas as pl
from jax.experimental.pallas import tpu as pltpu
from jax.sharding import PartitionSpec as P

CLU_DEV = 8
SLOTS = 4
MESH = pl.DeviceIdType.MESH
F32 = jnp.float32
BF16 = jnp.bfloat16
NN = (((1,), (0,)), ((), ()))
NT = (((1,), (1,)), ((), ()))
TN = (((0,), (0,)), ((), ()))


def dot(a, b, dims=NN):
    return lax.dot_general(a, b, dims, preferred_element_type=F32)


def iota(shape, dim):
    return lax.broadcasted_iota(jnp.int32, shape, dim)


def kernel(
    dims,
    q_hbm,
    k_hbm,
    v_hbm,
    cid_hbm,
    w_hbm,
    go_hbm,
    mixed_ref,
    dq_ref,
    dk_ref,
    dv_ref,
    cid_ref,
    w_ref,
    xcat,
    pack,
    unpack,
    msnd,
    mrcv,
    snd1,
    rcv1,
    sndg,
    rcvg,
    snda,
    rcva,
    sndb,
    rcvb,
    grads_in,
    wt,
    gout,
    rsnd,
    rrcv,
    cells,
    probs,
    outs,
    ssem,
    rsem,
    lsem,
):
    ny, nx, nt, heads, tok, dh = dims
    ns = ny * nx * 2
    hb = heads // 2
    blk = hb * SLOTS
    peers = min(32, ns)
    chunks = ns // peers
    rows = peers * blk
    part = peers * SLOTS
    recv_rows = ns * SLOTS
    half = hb * dh
    columns = nx * 2 * 32
    scale = 1.0 / math.sqrt(dh)
    me = lax.axis_index("seq")
    mt = lax.axis_index("tensor")
    my = lax.div(me, 2 * nx)
    mx = lax.rem(lax.div(me, 2), nx)
    mc = lax.rem(me, 2)

    loads = [
        pltpu.make_async_copy(cid_hbm, cid_ref, lsem.at[0]),
        pltpu.make_async_copy(w_hbm, w_ref, lsem.at[1]),
        pltpu.make_async_copy(go_hbm, gout.at[mt], lsem.at[2]),
    ]
    for t, ref in enumerate((q_hbm, k_hbm, v_hbm)):
        for h in range(heads):
            loads.append(
                pltpu.make_async_copy(
                    ref.at[:, pl.ds(h * dh, dh)],
                    xcat.at[h // hb, pl.ds(h % hb * tok, tok), pl.ds(t * dh, dh)],
                    lsem.at[3 + t * heads + h],
                )
            )
    for load in loads:
        load.start()

    barrier = pltpu.get_barrier_semaphore()

    def greet_seq(j, carry):
        pl.semaphore_signal(
            barrier, inc=1, device_id={"seq": lax.rem(me + j, ns)}, device_id_type=MESH
        )
        return carry

    lax.fori_loop(1, ns, greet_seq, 0)

    def greet_tensor(j, carry):
        pl.semaphore_signal(
            barrier, inc=1, device_id={"tensor": lax.rem(mt + j, nt)}, device_id_type=MESH
        )
        return carry

    lax.fori_loop(1, nt, greet_tensor, 0)

    def remote(src, dst, index, target):
        return pltpu.make_async_remote_copy(
            src_ref=src,
            dst_ref=dst,
            send_sem=ssem.at[index],
            recv_sem=rsem.at[index],
            device_id=target,
            device_id_type=MESH,
        )

    def wait_recv(ref, index):
        pltpu.make_async_copy(ref, ref, rsem.at[index]).wait()

    def wait_send(ref, index):
        pltpu.make_async_copy(ref, ref, ssem.at[index]).wait()

    def exchange(src, dst, index):
        def step(j, carry):
            ahead = lax.rem(me + j, ns)
            behind = lax.rem(me + ns - j, ns)
            remote(src.at[ahead], dst.at[me], index, {"seq": ahead}).start()
            remote(src.at[behind], dst.at[me], index, {"seq": behind}).start()
            return carry

        far = lax.rem(me + ns // 2, ns)
        remote(src.at[far], dst.at[me], index, {"seq": far}).start()
        lax.fori_loop(1, ns // 2, step, 0)

    def send_rows(snd, rcv, i, index):
        exchange(snd.at[i], rcv.at[i], index + i)
        rcv[i, me] = snd[i, me]

    def wait_rows(rcv, i, index):
        wait_recv(rcv.at[i, pl.ds(0, ns - 1)], index + i)

    def flat(block):
        return block.astype(F32).reshape(-1, dh).astype(BF16)

    def tiles(values):
        return values.reshape(-1, blk, dh).astype(BF16)

    loads[0].wait()
    upper = (iota((tok, tok), 0) < iota((tok, tok), 1)).astype(BF16)
    diag = iota((tok, tok), 0) == iota((tok, tok), 1)
    table = jnp.zeros((ns, 128), F32)
    dests = []
    for h in range(heads):
        cid = cid_ref[h : h + 1, :]
        owner = lax.shift_right_logical(cid, 3)
        member = iota((ns, tok), 0) == owner
        onehot = member.astype(F32)
        earlier = dot(onehot.astype(BF16), upper)
        rank = jnp.sum(onehot * earlier, axis=0, keepdims=True).astype(jnp.int32)
        i, g = divmod(h, hb)
        dest = owner * blk + g * SLOTS + rank
        dests.append(dest)
        for c in range(chunks):
            pack[i, c, :, g * tok : (g + 1) * tok] = (
                iota((rows, tok), 0) + c * rows == dest
            ).astype(BF16)
        value = jnp.where(member, (cid & (CLU_DEV - 1)) + 1, 0).astype(F32).astype(BF16)
        lane = (iota((128, tok), 0) == rank + h * SLOTS).astype(BF16)
        table = table + dot(value, lane, NT)
    msnd[...] = table.reshape(ns, 1, 128)

    loads[1].wait()
    block = dot((iota((32, 32), 0) == iota((32, 32), 1)).astype(BF16), w_ref[...], NT)
    for i in range(2):
        wt[i, my, mx, mc] = block[:, i * half : (i + 1) * half].astype(BF16)

    for i in range(2):
        for t in range(3):
            for h in range(i * hb, (i + 1) * hb):
                loads[3 + t * heads + h].wait()
        for c in range(chunks):
            packed = dot(pack[i, c], xcat[i])
            for t in range(3):
                snd1[i, c * peers : (c + 1) * peers, t] = tiles(packed[:, t * dh : (t + 1) * dh])
    loads[2].wait()

    pl.semaphore_wait(barrier, ns - 1 + nt - 1)

    def weight_y(i):
        def step(j, carry):
            target = (lax.rem(my + j, ny) * nx + mx) * 2 + mc
            remote(
                wt.at[i, my, mx, mc], wt.at[i, my, mx, mc], 8 + i, {"seq": target}
            ).start()
            return carry

        lax.fori_loop(1, ny, step, 0)

    def weight_x(i):
        wait_recv(wt.at[i, pl.ds(0, ny - 1), 0, 0], 8 + i)

        def step(j, carry):
            target = (my * nx + lax.rem(mx + j, nx)) * 2 + mc
            remote(wt.at[i, :, mx, mc], wt.at[i, :, mx, mc], 10 + i, {"seq": target}).start()
            return carry

        lax.fori_loop(1, nx, step, 0)

    def weight_core(i):
        wait_recv(wt.at[i, :, pl.ds(0, nx - 1), 0], 10 + i)
        remote(
            wt.at[i, :, :, mc], wt.at[i, :, :, mc], 12 + i, {"seq": me + 1 - 2 * mc}
        ).start()

    weight_y(0)
    weight_y(1)

    def cotangent(j, carry):
        remote(gout.at[mt], gout.at[mt], 14, {"tensor": lax.rem(mt + j, nt)}).start()
        return carry

    lax.fori_loop(1, nt, cotangent, 0)

    exchange(msnd, mrcv, 15)
    mrcv[me] = msnd[me]
    send_rows(snd1, rcv1, 0, 0)
    weight_x(0)
    weight_x(1)
    send_rows(snd1, rcv1, 1, 0)

    for h in range(heads):
        column = jnp.sum(
            jnp.where(diag, dests[h], 0).astype(F32), axis=1, keepdims=True
        ).astype(jnp.int32)
        unpack[h] = (iota((tok, ns * blk), 1) == column).astype(BF16)

    def source(index):
        h = lax.div(index, part)
        rest = index - h * part
        p = lax.div(rest, SLOTS)
        return p * blk + h * SLOTS + (rest - p * SLOTS)

    to_heads = (source(iota((rows, 1), 0)) == iota((rows, rows), 1)).astype(BF16)
    to_peers = (source(iota((1, rows), 1)) == iota((rows, rows), 0)).astype(BF16)
    lanes = iota((rows, 128), 1)

    def grad_rows(i):
        wait_recv(wt.at[i, :, :, 0], 12 + i)
        grad = jnp.zeros((tok, half), F32)
        for y in range(ny):
            grad = grad + dot(
                gout[:, :, y * columns : (y + 1) * columns].reshape(tok, columns),
                wt[i, y].reshape(columns, half),
            )
        grad = grad.astype(BF16)
        for g in range(hb):
            grads_in[i, g * tok : (g + 1) * tok] = grad[:, g * dh : (g + 1) * dh]
        for c in range(chunks):
            sndg[i, c * peers : (c + 1) * peers] = tiles(dot(pack[i, c], grads_in[i]))
        send_rows(sndg, rcvg, i, 2)

    def by_head(i, c, values, slots):
        moved = dot(to_heads, values).astype(BF16)
        for n, slot in enumerate(slots):
            for g in range(hb):
                cells[slot, i * hb + g, c] = moved[
                    g * part : (g + 1) * part, n * dh : (n + 1) * dh
                ]

    def cell(index, h):
        return cells[index, h].reshape(recv_rows, dh)

    def keep(index, h, value):
        outs[index, h] = value.astype(BF16).reshape(chunks, part, dh)

    def by_peer(i, c, indices):
        return dot(
            to_peers,
            jnp.concatenate(
                [
                    jnp.concatenate([outs[n, i * hb + g, c] for g in range(hb)], axis=0)
                    for n in indices
                ],
                axis=1,
            ),
        )

    def forward(i):
        wait_rows(rcv1, i, 0)
        for c in range(chunks):
            here = slice(c * peers, (c + 1) * peers)
            spread = jnp.broadcast_to(mrcv[here], (peers, blk, 128)).reshape(rows, 128)
            own_lane = lanes == (iota((rows, 128), 0) & (blk - 1)) + i * blk
            mark = jnp.sum(jnp.where(own_lane, spread, 0.0), axis=1, keepdims=True)
            marks = ((lanes.astype(F32) == mark) & (lanes > 0)).astype(BF16)
            values = [flat(rcv1[i, here, t]) for t in range(3)]
            by_head(i, c, jnp.concatenate(values + [marks], axis=1), (0, 1, 2, 4))
        for h in range(i * hb, (i + 1) * hb):
            marks = cell(4, h)
            same = dot(marks, marks, NT) > 0.5
            scores = jnp.where(same, dot(cell(0, h), cell(1, h), NT) * scale, -1e30)
            weights = jnp.exp(scores - jnp.max(scores, axis=1, keepdims=True))
            prob = weights / jnp.sum(weights, axis=1, keepdims=True)
            probs[h] = prob
            keep(0, h, dot(prob.astype(BF16), cell(2, h)))
        for c in range(chunks):
            snda[i, c * peers : (c + 1) * peers] = tiles(by_peer(i, c, (0,)))
        send_rows(snda, rcva, i, 4)

    def backward(i):
        wait_rows(rcvg, i, 2)
        for c in range(chunks):
            by_head(i, c, flat(rcvg[i, c * peers : (c + 1) * peers]), (3,))
        for h in range(i * hb, (i + 1) * hb):
            grads = cell(3, h)
            prob = probs[h]
            attended = outs[0, h].reshape(recv_rows, dh)
            delta = jnp.sum(grads.astype(F32) * attended.astype(F32), axis=1, keepdims=True)
            grad_probs = dot(grads, cell(2, h), NT)
            grad_scores = (prob * (grad_probs - delta)).astype(BF16)
            keep(1, h, dot(grad_scores, cell(1, h)) * scale)
            keep(2, h, dot(grad_scores, cell(0, h), TN) * scale)
            keep(3, h, dot(prob.astype(BF16), grads, TN))
        for c in range(chunks):
            back = by_peer(i, c, (1, 2, 3))
            for t in range(3):
                sndb[i, c * peers : (c + 1) * peers, t] = tiles(back[:, t * dh : (t + 1) * dh])
        send_rows(sndb, rcvb, i, 6)

    weight_core(0)
    wait_recv(gout.at[pl.ds(0, nt - 1)], 14)
    grad_rows(0)
    weight_core(1)
    wait_recv(mrcv.at[pl.ds(0, ns - 1)], 15)
    forward(0)
    grad_rows(1)
    forward(1)
    backward(0)
    backward(1)

    attended = []
    for i in range(2):
        wait_rows(rcva, i, 4)
        arrived = flat(rcva[i])
        attended.append(
            jnp.concatenate(
                [dot(unpack[h], arrived).astype(BF16) for h in range(i * hb, (i + 1) * hb)],
                axis=1,
            )
        )

    def project(y, carry):
        rsnd[:, y] = (
            (
                dot(attended[0], wt[0, y].reshape(columns, half), NT)
                + dot(attended[1], wt[1, y].reshape(columns, half), NT)
            )
            .astype(BF16)
            .reshape(nt, tok // nt, columns)
        )

        def scatter(j, inner):
            target = lax.rem(mt + j, nt)
            remote(rsnd.at[target, y], rrcv.at[mt, y], 16, {"tensor": target}).start()
            return inner

        lax.fori_loop(1, nt, scatter, 0)
        rrcv[mt, y] = rsnd[mt, y]
        return carry

    lax.fori_loop(0, ny, project, 0)

    def deliver(i):
        wait_rows(rcvb, i, 6)
        arrived = jnp.concatenate([flat(rcvb[i, :, t]) for t in range(3)], axis=1)
        for h in range(i * hb, (i + 1) * hb):
            back = dot(unpack[h], arrived).astype(BF16)
            for t, ref in enumerate((dq_ref, dk_ref, dv_ref)):
                ref[:, h * dh : (h + 1) * dh] = back[:, t * dh : (t + 1) * dh]

    deliver(0)
    wait_recv(rrcv.at[pl.ds(0, nt - 1)], 16)
    for y in range(ny):
        total = rrcv[0, y].astype(F32)
        for t in range(1, nt):
            total = total + rrcv[t, y].astype(F32)
        mixed_ref[:, y * columns : (y + 1) * columns] = total.astype(BF16)
    deliver(1)

    for i in range(2):
        wait_send(wt.at[i, pl.ds(0, ny - 1), 0, 0], 8 + i)
        wait_send(wt.at[i, :, pl.ds(0, nx - 1), 0], 10 + i)
        wait_send(wt.at[i, :, :, 0], 12 + i)
    wait_send(gout.at[pl.ds(0, nt - 1)], 14)
    wait_send(msnd.at[pl.ds(0, ns - 1)], 15)
    wait_send(rsnd.at[pl.ds(0, nt - 1)], 16)
    for i in range(2):
        for n, ref in enumerate((snd1, sndg, snda, sndb)):
            wait_send(ref.at[i, pl.ds(0, ns - 1)], 2 * n + i)


def solution(mesh, grid=(8, 4)):
    ny, nx = grid
    ns, nt = mesh.shape["seq"], mesh.shape["tensor"]

    def shards(query_rows, key_rows, value_rows, cluster_id, slot_index, out_weight, grad_out):
        tok = query_rows.shape[0]
        heads = cluster_id.shape[0]
        dh = query_rows.shape[1] // heads
        hb = heads // 2
        blk = hb * SLOTS
        peers = min(32, ns)
        chunks = ns // peers
        rows = peers * blk
        part = peers * SLOTS
        columns = nx * 2 * 32
        vmem = pl.BlockSpec(memory_space=pltpu.VMEM)
        one = pltpu.VMEM((2, ns, blk, dh), BF16)
        three = pltpu.VMEM((2, ns, 3, blk, dh), BF16)
        wide = jax.ShapeDtypeStruct(query_rows.shape, BF16)
        return pl.pallas_call(
            functools.partial(kernel, (ny, nx, nt, heads, tok, dh)),
            out_shape=(jax.ShapeDtypeStruct(grad_out.shape, BF16), wide, wide, wide),
            in_specs=[pl.BlockSpec(memory_space=pltpu.HBM)] * 6,
            out_specs=(vmem,) * 4,
            scratch_shapes=[
                pltpu.VMEM(cluster_id.shape, jnp.int32),
                pltpu.VMEM(out_weight.shape, BF16),
                pltpu.VMEM((2, hb * tok, 3 * dh), BF16),
                pltpu.VMEM((2, chunks, rows, hb * tok), BF16),
                pltpu.VMEM((heads, tok, ns * blk), BF16),
                pltpu.VMEM((ns, 1, 128), F32),
                pltpu.VMEM((ns, 1, 128), F32),
                three,
                three,
                one,
                one,
                one,
                one,
                three,
                three,
                pltpu.VMEM((2, hb * tok, dh), BF16),
                pltpu.VMEM((2, ny, nx, 2, 32, heads * dh // 2), BF16),
                pltpu.VMEM((nt,) + grad_out.shape, BF16),
                pltpu.VMEM((nt, ny, tok // nt, columns), BF16),
                pltpu.VMEM((nt, ny, tok // nt, columns), BF16),
                pltpu.VMEM((5, heads, chunks, part, dh), BF16),
                pltpu.VMEM((heads, ns * SLOTS, ns * SLOTS), F32),
                pltpu.VMEM((4, heads, chunks, part, dh), BF16),
                pltpu.SemaphoreType.DMA((17,)),
                pltpu.SemaphoreType.DMA((17,)),
                pltpu.SemaphoreType.DMA((3 + 3 * heads,)),
            ],
            compiler_params=pltpu.CompilerParams(
                collective_id=0, has_side_effects=True, vmem_limit_bytes=48 * 1024 * 1024
            ),
        )(query_rows, key_rows, value_rows, cluster_id, out_weight, grad_out)

    return jax.shard_map(
        shards,
        mesh=mesh,
        in_specs=(
            P("seq", "tensor"),
            P("seq", "tensor"),
            P("seq", "tensor"),
            P("tensor", "seq"),
            P("tensor", "seq"),
            P("tensor", "seq"),
            P(("seq", "tensor"), None),
        ),
        out_specs=(
            P(("seq", "tensor"), None),
            P("seq", "tensor"),
            P("seq", "tensor"),
            P("seq", "tensor"),
        ),
        check_vma=False,
    )
```

time: 88 us -> 81.1 us (0.922)
  Pallas kernels: 80.5 us -> 74 us
    pallas_call x1, Pallas kernels: 80.5 us -> 74 us  [shards(): pl.pallas_call(functools.partial(kernel, (ny, nx, nt, heads, tok, dh)), o...]
where the time goes in v2:
time: 81.1 us; the launch traced here: 80.8 us
  Pallas kernels  74 us (91%)
  local copies, waits for them, and re-layouts  6.16 us (8%)
    pallas_call x1, Pallas kernels, shards(): pl.pallas_call(functools.partial(kernel, (ny, nx, nt, heads, tok, dh)), o...  74 us
    unnamed x15, local copies, waits for them, and re-layouts  6.16 us

profile of v2, /device:TPU:1, one launch (start us, length us, event | category | flops | bytes accessed | tf_op | source)
XLA Modules:
  0.0 80.8 jit_solution(1255272301916028844)
XLA Ops:
  0.6 0.0 copy-start.4
  0.6 0.0 copy-start
  0.7 0.9 %copy.10.w_hbm = bf16[512,32]{1,0:T(8,128)(2,1)S(1)} copy(bf16[512,32]{0,1:T(8,128)(2,1)} %param.11) | data formatting | bytes 65536 | tf_op args[5]
  1.6 0.0 copy-done.4
  1.6 0.0 copy-done
  1.6 0.0 copy-start.1
  1.6 0.9 %copy-done.1 = bf16[128,512]{1,0:T(8,128)(2,1)S(1)} copy-done((bf16[128,512]{1,0:T(8,128)(2,1)S(1)}, bf16[128,512]{1,0:T(8,128)(2,1)}, u32[]{:S(2)}) %copy-start.1) | copy-done | bytes 131096
  2.5 0.0 copy-start.2
  2.5 0.9 %copy-done.2 = bf16[128,512]{1,0:T(8,128)(2,1)S(1)} copy-done((bf16[128,512]{1,0:T(8,128)(2,1)S(1)}, bf16[128,512]{1,0:T(8,128)(2,1)}, u32[]{:S(2)}) %copy-start.2) | copy-done | bytes 131096
  3.4 0.0 copy-start.3
  3.4 0.8 %copy-done.3 = bf16[16,2048]{1,0:T(8,128)(2,1)S(1)} copy-done((bf16[16,2048]{1,0:T(8,128)(2,1)S(1)}, bf16[16,2048]{1,0:T(8,128)(2,1)}, u32[]{:S(2)}) %copy-start.3) | copy-done | bytes 65560
  4.2 74.0 %shard_map.93 = (bf16[16,2048]{1,0:T(8,128)(2,1)S(1)}, bf16[128,512]{1,0:T(8,128)(2,1)S(1)}, bf16[128,512]{1,0:T(8,128)(2,1)S(1)}, bf16[128,512]{1,0:T(8,128)(2,1)S(1)}) custom-call(bf16[128,512]{1,0:T(8,128)(2,1)S(1)} %copy-done, bf16[128,512]{1,0:T(8,128)(2,1)S(1)} %copy-done.1, bf16[128,512]{1,0:T(8,128)(2,1)S(1)} %copy-done.2, s32[4,128]{1,0:T(4,128)S(1)} %copy-done.4, ...), custom_call_target="tpu_custom_call" | custom-call | tf_op jit(solution)/shard_map/pallas_call | solution.py:435
  78.2 0.6 copy.15
  78.9 0.7 copy.16
  79.5 0.7 copy.17
  80.2 0.7 copy.18
Async XLA Ops:
  0.6 0.9 %copy-start.4 = (s32[4,128]{1,0:T(4,128)S(1)}, s32[4,128]{1,0:T(4,128)}, u32[]{:S(2)}) copy-start(s32[4,128]{1,0:T(4,128)} %cid_hbm.1) | copy-start | bytes 6148
  0.6 0.9 %copy-start = (bf16[128,512]{1,0:T(8,128)(2,1)S(1)}, bf16[128,512]{1,0:T(8,128)(2,1)}, u32[]{:S(2)}) copy-start(bf16[128,512]{1,0:T(8,128)(2,1)} %q_hbm.1) | copy-start | bytes 393220
  1.6 0.9 %copy-start.1 = (bf16[128,512]{1,0:T(8,128)(2,1)S(1)}, bf16[128,512]{1,0:T(8,128)(2,1)}, u32[]{:S(2)}) copy-start(bf16[128,512]{1,0:T(8,128)(2,1)} %k_hbm.1) | copy-start | bytes 393220
  2.5 0.9 %copy-start.2 = (bf16[128,512]{1,0:T(8,128)(2,1)S(1)}, bf16[128,512]{1,0:T(8,128)(2,1)}, u32[]{:S(2)}) copy-start(bf16[128,512]{1,0:T(8,128)(2,1)} %v_hbm.1) | copy-start | bytes 393220
  3.4 0.8 %copy-start.3 = (bf16[16,2048]{1,0:T(8,128)(2,1)S(1)}, bf16[16,2048]{1,0:T(8,128)(2,1)}, u32[]{:S(2)}) copy-start(bf16[16,2048]{1,0:T(8,128)(2,1)} %go_hbm.1) | copy-start | bytes 196612

commit v3 on v2

--- a/solution.py
+++ b/solution.py
@@ -238,9 +238,9 @@
     exchange(msnd, mrcv, 15)
     mrcv[me] = msnd[me]
     send_rows(snd1, rcv1, 0, 0)
+    send_rows(snd1, rcv1, 1, 0)
     weight_x(0)
     weight_x(1)
-    send_rows(snd1, rcv1, 1, 0)
 
     for h in range(heads):
         column = jnp.sum(
@@ -342,16 +342,14 @@
         send_rows(sndb, rcvb, i, 6)
 
     weight_core(0)
+    wait_recv(mrcv.at[pl.ds(0, ns - 1)], 15)
+    forward(0)
     wait_recv(gout.at[pl.ds(0, nt - 1)], 14)
     grad_rows(0)
     weight_core(1)
-    wait_recv(mrcv.at[pl.ds(0, ns - 1)], 15)
-    forward(0)
+    forward(1)
     grad_rows(1)
-    forward(1)
     backward(0)
-    backward(1)
-
     attended = []
     for i in range(2):
         wait_rows(rcva, i, 4)
@@ -383,6 +381,8 @@
         return carry
 
     lax.fori_loop(0, ny, project, 0)
+
+    backward(1)
 
     def deliver(i):
         wait_rows(rcvb, i, 6)

time: 81.1 us -> 78.8 us (0.972)
  Pallas kernels: 74 us -> 71.7 us
    pallas_call x1, Pallas kernels: 74 us -> 71.7 us  [shards(): pl.pallas_call(functools.partial(kernel, (ny, nx, nt, heads, tok, dh)), o...]
where the time goes in v3:
time: 78.8 us; the launch traced here: 78.6 us
  Pallas kernels  71.7 us (91%)
  local copies, waits for them, and re-layouts  6.16 us (8%)
    pallas_call x1, Pallas kernels, shards(): pl.pallas_call(functools.partial(kernel, (ny, nx, nt, heads, tok, dh)), o...  71.7 us
    unnamed x15, local copies, waits for them, and re-layouts  6.16 us

profile of v3, /device:TPU:1, one launch (start us, length us, event | category | flops | bytes accessed | tf_op | source)
XLA Modules:
  0.0 78.6 jit_solution(13537604954195790416)
XLA Ops:
  0.6 0.0 copy-start.4
  0.6 0.0 copy-start
  0.7 0.9 %copy.10.w_hbm = bf16[512,32]{1,0:T(8,128)(2,1)S(1)} copy(bf16[512,32]{0,1:T(8,128)(2,1)} %param.11) | data formatting | bytes 65536 | tf_op args[5]
  1.6 0.0 copy-done.4
  1.6 0.0 copy-done
  1.6 0.0 copy-start.1
  1.6 0.9 %copy-done.1 = bf16[128,512]{1,0:T(8,128)(2,1)S(1)} copy-done((bf16[128,512]{1,0:T(8,128)(2,1)S(1)}, bf16[128,512]{1,0:T(8,128)(2,1)}, u32[]{:S(2)}) %copy-start.1) | copy-done | bytes 131096
  2.5 0.0 copy-start.2
  2.5 0.9 %copy-done.2 = bf16[128,512]{1,0:T(8,128)(2,1)S(1)} copy-done((bf16[128,512]{1,0:T(8,128)(2,1)S(1)}, bf16[128,512]{1,0:T(8,128)(2,1)}, u32[]{:S(2)}) %copy-start.2) | copy-done | bytes 131096
  3.4 0.0 copy-start.3
  3.4 0.8 %copy-done.3 = bf16[16,2048]{1,0:T(8,128)(2,1)S(1)} copy-done((bf16[16,2048]{1,0:T(8,128)(2,1)S(1)}, bf16[16,2048]{1,0:T(8,128)(2,1)}, u32[]{:S(2)}) %copy-start.3) | copy-done | bytes 65560
  4.2 71.7 %shard_map.93 = (bf16[16,2048]{1,0:T(8,128)(2,1)S(1)}, bf16[128,512]{1,0:T(8,128)(2,1)S(1)}, bf16[128,512]{1,0:T(8,128)(2,1)S(1)}, bf16[128,512]{1,0:T(8,128)(2,1)S(1)}) custom-call(bf16[128,512]{1,0:T(8,128)(2,1)S(1)} %copy-done, bf16[128,512]{1,0:T(8,128)(2,1)S(1)} %copy-done.1, bf16[128,512]{1,0:T(8,128)(2,1)S(1)} %copy-done.2, s32[4,128]{1,0:T(4,128)S(1)} %copy-done.4, ...), custom_call_target="tpu_custom_call" | custom-call | tf_op jit(solution)/shard_map/pallas_call | solution.py:435
  76.0 0.6 copy.15
  76.6 0.7 copy.16
  77.3 0.7 copy.17
  77.9 0.7 copy.18
Async XLA Ops:
  0.6 0.9 %copy-start.4 = (s32[4,128]{1,0:T(4,128)S(1)}, s32[4,128]{1,0:T(4,128)}, u32[]{:S(2)}) copy-start(s32[4,128]{1,0:T(4,128)} %cid_hbm.1) | copy-start | bytes 6148
  0.6 0.9 %copy-start = (bf16[128,512]{1,0:T(8,128)(2,1)S(1)}, bf16[128,512]{1,0:T(8,128)(2,1)}, u32[]{:S(2)}) copy-start(bf16[128,512]{1,0:T(8,128)(2,1)} %q_hbm.1) | copy-start | bytes 393220
  1.6 0.9 %copy-start.1 = (bf16[128,512]{1,0:T(8,128)(2,1)S(1)}, bf16[128,512]{1,0:T(8,128)(2,1)}, u32[]{:S(2)}) copy-start(bf16[128,512]{1,0:T(8,128)(2,1)} %k_hbm.1) | copy-start | bytes 393220
  2.5 0.9 %copy-start.2 = (bf16[128,512]{1,0:T(8,128)(2,1)S(1)}, bf16[128,512]{1,0:T(8,128)(2,1)}, u32[]{:S(2)}) copy-start(bf16[128,512]{1,0:T(8,128)(2,1)} %v_hbm.1) | copy-start | bytes 393220
  3.4 0.8 %copy-start.3 = (bf16[16,2048]{1,0:T(8,128)(2,1)S(1)}, bf16[16,2048]{1,0:T(8,128)(2,1)}, u32[]{:S(2)}) copy-start(bf16[16,2048]{1,0:T(8,128)(2,1)} %go_hbm.1) | copy-start | bytes 196612

commit v4 on v3

--- a/solution.py
+++ b/solution.py
@@ -102,13 +102,18 @@
 
     barrier = pltpu.get_barrier_semaphore()
 
+    def greet(peer):
+        pl.semaphore_signal(
+            barrier, inc=1, device_id={"seq": lax.rem(peer, ns)}, device_id_type=MESH
+        )
+
     def greet_seq(j, carry):
-        pl.semaphore_signal(
-            barrier, inc=1, device_id={"seq": lax.rem(me + j, ns)}, device_id_type=MESH
-        )
+        greet(me + ns // 2 + j)
+        greet(me + ns // 2 - j)
         return carry
 
-    lax.fori_loop(1, ns, greet_seq, 0)
+    greet(me + ns // 2)
+    lax.fori_loop(1, ns // 2, greet_seq, 0)
 
     def greet_tensor(j, carry):
         pl.semaphore_signal(
@@ -136,8 +141,8 @@
 
     def exchange(src, dst, index):
         def step(j, carry):
-            ahead = lax.rem(me + j, ns)
-            behind = lax.rem(me + ns - j, ns)
+            ahead = lax.rem(me + ns // 2 + j, ns)
+            behind = lax.rem(me + ns // 2 - j, ns)
             remote(src.at[ahead], dst.at[me], index, {"seq": ahead}).start()
             remote(src.at[behind], dst.at[me], index, {"seq": behind}).start()
             return carry

time: 78.8 us -> 77.5 us (0.984)
  Pallas kernels: 71.7 us -> 70.4 us
    pallas_call x1, Pallas kernels: 71.7 us -> 70.4 us  [shards(): pl.pallas_call(functools.partial(kernel, (ny, nx, nt, heads, tok, dh)), o...]
where the time goes in v4:
time: 77.5 us; the launch traced here: 77.3 us
  Pallas kernels  70.4 us (91%)
  local copies, waits for them, and re-layouts  6.16 us (8%)
    pallas_call x1, Pallas kernels, shards(): pl.pallas_call(functools.partial(kernel, (ny, nx, nt, heads, tok, dh)), o...  70.4 us
    unnamed x15, local copies, waits for them, and re-layouts  6.16 us

profile of v4, /device:TPU:1, one launch (start us, length us, event | category | flops | bytes accessed | tf_op | source)
XLA Modules:
  0.0 77.3 jit_solution(5352553614880964453)
XLA Ops:
  0.6 0.0 copy-start.4
  0.6 0.0 copy-start
  0.7 0.9 %copy.10.w_hbm = bf16[512,32]{1,0:T(8,128)(2,1)S(1)} copy(bf16[512,32]{0,1:T(8,128)(2,1)} %param.11) | data formatting | bytes 65536 | tf_op args[5]
  1.6 0.0 copy-done.4
  1.6 0.0 copy-done
  1.6 0.0 copy-start.1
  1.6 0.9 %copy-done.1 = bf16[128,512]{1,0:T(8,128)(2,1)S(1)} copy-done((bf16[128,512]{1,0:T(8,128)(2,1)S(1)}, bf16[128,512]{1,0:T(8,128)(2,1)}, u32[]{:S(2)}) %copy-start.1) | copy-done | bytes 131096
  2.5 0.0 copy-start.2
  2.5 0.9 %copy-done.2 = bf16[128,512]{1,0:T(8,128)(2,1)S(1)} copy-done((bf16[128,512]{1,0:T(8,128)(2,1)S(1)}, bf16[128,512]{1,0:T(8,128)(2,1)}, u32[]{:S(2)}) %copy-start.2) | copy-done | bytes 131096
  3.4 0.0 copy-start.3
  3.4 0.8 %copy-done.3 = bf16[16,2048]{1,0:T(8,128)(2,1)S(1)} copy-done((bf16[16,2048]{1,0:T(8,128)(2,1)S(1)}, bf16[16,2048]{1,0:T(8,128)(2,1)}, u32[]{:S(2)}) %copy-start.3) | copy-done | bytes 65560
  4.2 70.4 %shard_map.93 = (bf16[16,2048]{1,0:T(8,128)(2,1)S(1)}, bf16[128,512]{1,0:T(8,128)(2,1)S(1)}, bf16[128,512]{1,0:T(8,128)(2,1)S(1)}, bf16[128,512]{1,0:T(8,128)(2,1)S(1)}) custom-call(bf16[128,512]{1,0:T(8,128)(2,1)S(1)} %copy-done, bf16[128,512]{1,0:T(8,128)(2,1)S(1)} %copy-done.1, bf16[128,512]{1,0:T(8,128)(2,1)S(1)} %copy-done.2, s32[4,128]{1,0:T(4,128)S(1)} %copy-done.4, ...), custom_call_target="tpu_custom_call" | custom-call | tf_op jit(solution)/shard_map/pallas_call | solution.py:440
  74.7 0.6 copy.15
  75.3 0.7 copy.16
  76.0 0.7 copy.17
  76.6 0.7 copy.18
Async XLA Ops:
  0.6 0.9 %copy-start.4 = (s32[4,128]{1,0:T(4,128)S(1)}, s32[4,128]{1,0:T(4,128)}, u32[]{:S(2)}) copy-start(s32[4,128]{1,0:T(4,128)} %cid_hbm.1) | copy-start | bytes 6148
  0.6 0.9 %copy-start = (bf16[128,512]{1,0:T(8,128)(2,1)S(1)}, bf16[128,512]{1,0:T(8,128)(2,1)}, u32[]{:S(2)}) copy-start(bf16[128,512]{1,0:T(8,128)(2,1)} %q_hbm.1) | copy-start | bytes 393220
  1.6 0.9 %copy-start.1 = (bf16[128,512]{1,0:T(8,128)(2,1)S(1)}, bf16[128,512]{1,0:T(8,128)(2,1)}, u32[]{:S(2)}) copy-start(bf16[128,512]{1,0:T(8,128)(2,1)} %k_hbm.1) | copy-start | bytes 393220
  2.5 0.9 %copy-start.2 = (bf16[128,512]{1,0:T(8,128)(2,1)S(1)}, bf16[128,512]{1,0:T(8,128)(2,1)}, u32[]{:S(2)}) copy-start(bf16[128,512]{1,0:T(8,128)(2,1)} %v_hbm.1) | copy-start | bytes 393220
  3.4 0.8 %copy-start.3 = (bf16[16,2048]{1,0:T(8,128)(2,1)S(1)}, bf16[16,2048]{1,0:T(8,128)(2,1)}, u32[]{:S(2)}) copy-start(bf16[16,2048]{1,0:T(8,128)(2,1)} %go_hbm.1) | copy-start | bytes 196612
